TPU v7x, 256 devices: a whole 4x4x8 slice. The times are simulated.
256 devices in a mesh: blk: 8 (over y_lo, x), tile: 32 (over y_hi, z, core).
Axes of the slice: x: 4, y: 4 (y_hi: 2, y_lo: 2; y = y_hi * 2 + y_lo), z: 8, core: 2. Of those that a mesh axis runs over, the one named last changes fastest.
Arguments:
- qkv: bfloat16 [3, 8192, 4096], P(None, ('blk', 'tile')), may hold values from -33 to 33
- frame_clip: int32 [16], replicated, may hold values from 0 to 2, never falling along the last dimension, each value on 1 to 10 neighbouring positions
- w_out: bfloat16 [4096, 5120], P('tile'), may hold values from -0.5 to 0.5
Outputs:
- projected: bfloat16 [8192, 5120], P(('blk', 'tile'))
All inputs are finite; a program needn't handle non-finite values.
Results may differ from a plain program's by a relative error of at most 0.023.
Values may be sent and summed in bfloat16 or wider, within the bound.
A program may use at most 64 MiB of HBM per device.

v0:
```python
import math
import jax
import jax.numpy as jnp
from jax import lax
from jax.sharding import PartitionSpec as P

FRB = 2
TPF = 16


def clip_lookup(frames, frame_clip):
    table = jnp.arange(frame_clip.shape[0], dtype=jnp.int32)
    hits = (frames[..., None] == table).astype(jnp.int32)
    return jnp.sum(hits * frame_clip, axis=-1)


def on_device(qkv, frame_clip, w_out):
    tiles = lax.axis_size("tile")
    blk_index = lax.axis_index("blk")
    tok_dev = qkv.shape[1]
    head_dim = w_out.shape[0]
    tok_blk = tok_dev * tiles
    scale = 1.0 / math.sqrt(head_dim)
    local = lax.all_to_all(qkv, "tile", split_axis=2, concat_axis=1, tiled=True)
    queries = local[0]
    keys_all = local[1]
    values_all = local[2]
    rows = jnp.arange(tok_blk, dtype=jnp.int32)
    query_clip = clip_lookup(blk_index * FRB + rows % tok_dev // TPF, frame_clip)
    start_state = (
        jnp.full((tok_blk,), -1e30, jnp.float32),
        jnp.zeros((tok_blk,), jnp.float32),
        jnp.zeros((tok_blk, head_dim), jnp.float32),
    )
    carry = start_state
    key_piece = lax.all_gather(keys_all, "blk", axis=0, tiled=True)
    value_piece = lax.all_gather(values_all, "blk", axis=0, tiled=True)
    count = key_piece.shape[0]
    width = math.gcd(count, tok_blk)
    key_blocks = key_piece.reshape(count // width, width, head_dim)
    value_blocks = value_piece.reshape(count // width, width, head_dim)
    firsts = width * jnp.arange(count // width, dtype=jnp.int32)

    def advance(state, item):
        key_block, value_block, first = item
        index = first + jnp.arange(width, dtype=jnp.int32)
        key_clip = clip_lookup(index // tok_blk * FRB + index % tok_dev // TPF, frame_clip)
        allowed = query_clip[:, None] == key_clip[None, :]
        run_max, run_sum, run_acc = state
        scores = (
            jnp.einsum("qd,kd->qk", queries, key_block, preferred_element_type=jnp.float32) * scale
        )
        masked = jnp.where(allowed, scores, -1e30)
        new_max = jnp.maximum(run_max, jnp.max(masked, axis=1))
        weights = jnp.where(allowed, jnp.exp(scores - new_max[:, None]), 0.0)
        factor = jnp.exp(run_max - new_max)
        new_sum = run_sum * factor + jnp.sum(weights, axis=1)
        new_acc = run_acc * factor[:, None] + jnp.dot(
            weights.astype(jnp.bfloat16), value_block, preferred_element_type=jnp.float32
        )
        state = (new_max, new_sum, new_acc)
        return (state, None)

    carry, unused = lax.scan(advance, carry, (key_blocks, value_blocks, firsts))
    run_max, run_sum, run_acc = carry
    attn = (run_acc / run_sum[:, None]).astype(jnp.bfloat16)
    return lax.psum_scatter(
        jnp.dot(attn, w_out, preferred_element_type=jnp.float32).astype(jnp.bfloat16),
        "tile",
        scatter_dimension=0,
        tiled=True,
    )


def solution(mesh):
    in_specs = (P(None, ("blk", "tile"), None), P(), P("tile", None))
    out_specs = P(("blk", "tile"), None)
    return jax.shard_map(
        on_device, mesh=mesh, in_specs=in_specs, out_specs=out_specs, check_vma=False
    )
```

profile of v0, /device:TPU:2, one launch (start us, length us, event | category | flops | bytes accessed | tf_op | source)
XLA Modules:
  0.0 374.8 jit_solution(4900958124774167915)
XLA Ops:
  6.5 6.1 %copy.17 = bf16[3,32,4096]{1,0,2:T(4,128)(2,1)} copy(bf16[3,32,4096]{2,1,0:T(8,128)(2,1)} %param.5) | data formatting | bytes 1572864 | tf_op args[0]
  12.6 6.2 %reshape.88 = bf16[32,2,6144]{2,1,0:T(2,128)(2,1)S(1)} reshape(bf16[4096,3,32]{2,1,0:T(4,128)(2,1)} %bitcast.49) | data formatting | bytes 1572864
  18.8 36.1 %all_to_all.15 = bf16[32,2,6144]{2,1,0:T(2,128)(2,1)S(1)} all-to-all(bf16[32,2,6144]{2,1,0:T(2,128)(2,1)S(1)} %reshape.88), channel_id=1, replica_groups=mesh['blk'=8,'tile'=32] {'tile'}, dimensions={0} | all-to-all | bytes 1572864 | tf_op jit(solution)/shard_map/all_to_all | solution.py:24
  55.0 4.9 %reshape.89 = bf16[4096,3,32]{2,1,0:T(4,128)(2,1)} reshape(bf16[32,2,6144]{2,1,0:T(2,128)(2,1)S(1)} %all_to_all.15) | data formatting | bytes 1572864
  59.8 4.2 %copy.22 = bf16[3,32,32,128]{3,2,1,0:T(8,128)(2,1)S(1)} copy(bf16[3,32,32,128]{1,0,3,2:T(4,128)(2,1)} %bitcast.48) | data formatting | bytes 1572864 | tf_op jit(solution)/shard_map/all_to_all | solution.py:24
  66.2 35.8 %all-gather.5.cloned.1.call-done = bf16[8192,128]{1,0:T(8,128)(2,1)} async-done(((bf16[1024,128]{1,0:T(8,128)(2,1)}), bf16[8192,128]{1,0:T(8,128)(2,1)}) %all-gather.5.cloned.1.call-update) | async-done | bytes 2097168 | tf_op jit(solution)/shard_map/all_gather | solution.py:37
  101.9 45.2 %all-gather.3.cloned.1.call-done = bf16[8192,128]{1,0:T(8,128)(2,1)} async-done(((bf16[1024,128]{1,0:T(8,128)(2,1)}), bf16[8192,128]{1,0:T(8,128)(2,1)}) %all-gather.3.cloned.1.call-update) | async-done | bytes 2097168 | tf_op jit(solution)/shard_map/all_gather | solution.py:36
  147.1 50.5 %while.18 = (s32[]{:T(128)}, f32[1024]{0:T(1024)S(1)}, f32[1024]{0:T(1024)S(1)}, f32[1024,128]{1,0:T(8,128)S(1)}, s32[1024]{0:T(1024)S(1)}, /*index=5*/s32[8]{0:...) while((s32[]{:T(128)}, f32[1024]{0:T(1024)S(1)}, ...), condition=%wide.region_5.6_spmd.clone, body=%wide.region_1.5_spmd.clone.sunk | while | flops 552039424 | bytes 14520545 | solution.py:64
  148.4 1.7 fusion.53
  151.2 2.2 fusion.56
  154.8 1.7 fusion.53
  157.5 2.2 fusion.56
  161.1 1.7 fusion.53
  163.8 2.2 fusion.56
  167.4 1.7 fusion.53
  170.1 2.2 fusion.56
  173.7 1.7 fusion.53
  176.4 2.2 fusion.56
  180.0 1.7 fusion.53
  182.7 2.2 fusion.56
  189.0 2.2 fusion.56
  195.3 2.2 fusion.56
  197.6 5.6 %convolution_convert_fusion = bf16[1024,5120]{1,0:T(8,128)(2,1)} fusion(bf16[128,5120]{1,0:T(8,128)(2,1)S(1)} %copy-done, f32[1024,128]{1,0:T(8,128)S(1)} %get-tuple-element.169, f32[1024]{0:T(1024)S(1)} %get-tuple-element.170), kind=kOutput, calls=%fused_computation.49 | convolution fusion | flops 1347682304 | bytes 12324864 | tf_op jit(solution)/shard_map/dot_general | solution.py:68
  203.2 165.0 %reduce-scatter.2.cloned.1.call-done = bf16[32,5120]{1,0:T(8,128)(2,1)} async-done(((bf16[1024,5120]{1,0:T(8,128)(2,1)}), bf16[32,5120]{1,0:T(8,128)(2,1)}) %reduce-scatter.2.cloned.1.call-update) | async-done | bytes 327696 | tf_op jit(solution)/shard_map/reduce_scatter | solution.py:67
  (78 shorter events, 24.0 us)
Async XLA Ops:
  6.5 191.0 %copy-start = (bf16[128,5120]{1,0:T(8,128)(2,1)S(1)}, bf16[128,5120]{1,0:T(8,128)(2,1)}, u32[]{:S(2)}) copy-start(bf16[128,5120]{1,0:T(8,128)(2,1)} %param.7) | copy-start | bytes 3932164
  6.5 95.4 %all-gather.5.cloned.1.call-start = ((), (), s32[]{:S(2)}) async-start(), calls=%async_computation.3 | async-start | bytes 2359296 | tf_op jit(solution)/shard_map/all_gather | solution.py:37
  59.8 6.1 %copy-start.1 = (s32[16]{0:T(128)S(1)}, s32[16]{0:T(128)}, u32[]{:S(2)}) copy-start(s32[16]{0:T(128)} %param.6) | copy-start | bytes 196
  64.9 82.2 %all-gather.3.cloned.1.call-start = ((), (), s32[]{:S(2)}) async-start(), calls=%async_computation.2 | async-start | bytes 2359296 | tf_op jit(solution)/shard_map/all_gather | solution.py:36
  65.8 302.4 %reduce-scatter.2.cloned.1.call-start = ((), (), s32[]{:S(2)}) async-start(), calls=%async_computation.4 | async-start | bytes 10813440 | tf_op jit(solution)/shard_map/reduce_scatter | solution.py:67
Sparse Core Ops, SparseCore 0:
  65.1 36.8 all-gather.4
  103.7 43.3 all-gather.2
  203.3 164.8 reduce-scatter.1
where the time goes:
time: 376 us; the launch traced here: 375 us
  waiting for transfers between devices  246 us (65%)
  matrix products  37 us (10%)
  blocking collectives  36.1 us (10%)
  local copies, waits for them, and re-layouts  27.9 us (7%)
  other arithmetic  14 us (4%)
  between operations  13.2 us (4%)
    reduce_scatter x1, waiting for transfers between devices, on_device(): lax.psum_scatter(jnp.dot(attn, w_out, preferred_element_type=jnp.float32)...  165 us
    all_gather x1, waiting for transfers between devices, on_device(): key_piece = lax.all_gather(keys_all, 'blk', axis=0, tiled=True)  45.2 us
    all_to_all x1, blocking collectives, on_device(): local = lax.all_to_all(qkv, 'tile', split_axis=2, concat_axis=1, tiled=True)  36.1 us
    all_gather x1, waiting for transfers between devices, on_device(): value_piece = lax.all_gather(values_all, 'blk', axis=0, tiled=True)  35.8 us
    dot_general x8, matrix products, advance(): jnp.dot(weights.astype(jnp.bfloat16), value_block, preferred_element_type...  17.7 us
    unnamed x7, local copies, waits for them, and re-layouts  17.2 us
    dot_general x8, matrix products, advance(): jnp.einsum('qd,kd->qk', queries, key_block, preferred_element_type=jnp.fl...  13.6 us
    reduce_sum x8, other arithmetic, advance(): new_sum = run_sum * factor + jnp.sum(weights, axis=1)  7.79 us
  transfers between devices with their start and end apart: 3, of which 3 were waited for; matrix products, arithmetic and copies ran while one was open for 0% of the time, Pallas kernels for 0%

commit v1 on v0

--- a/solution.py
+++ b/solution.py
@@ -33,8 +33,9 @@
         jnp.zeros((tok_blk, head_dim), jnp.float32),
     )
     carry = start_state
-    key_piece = lax.all_gather(keys_all, "blk", axis=0, tiled=True)
-    value_piece = lax.all_gather(values_all, "blk", axis=0, tiled=True)
+    spare = jnp.concatenate([keys_all, values_all], 1)
+    carry_in = lax.all_gather(spare, "blk", axis=0, tiled=True)
+    key_piece, value_piece = jnp.split(carry_in, [keys_all.shape[1]], axis=1)
     count = key_piece.shape[0]
     width = math.gcd(count, tok_blk)
     key_blocks = key_piece.reshape(count // width, width, head_dim)

time: 376 us -> 349 us (0.928)
  waiting for transfers between devices: 246 us -> 212 us
  local copies, waits for them, and re-layouts: 27.9 us -> 38 us
    all_gather x2 -> x1, waiting for transfers between devices: 80.9 us -> 47.2 us  [on_device(): carry_in = lax.all_gather(spare, 'blk', axis=0, tiled=True)]
    while x8 -> x40, local copies, waits for them, and re-layouts: 0.02 us -> 6.53 us
    dot_general x8, matrix products: 17.7 us -> 12 us  [advance(): jnp.dot(weights.astype(jnp.bfloat16), value_block, preferred_element_type...]
    split x0 -> x1, local copies, waits for them, and re-layouts: none -> 3.82 us  [on_device(): key_piece, value_piece = jnp.split(carry_in, [keys_all.shape[1]], axis=1)]
  transfers between devices with their start and end apart: 3 -> 2, of which waited for: 3 -> 2; matrix products, arithmetic and copies ran while one was open for 0% -> 0% of each run, Pallas kernels for 0% -> 0%
where the time goes in v1:
time: 349 us; the launch traced here: 348 us
  waiting for transfers between devices  212 us (61%)
  local copies, waits for them, and re-layouts  38 us (11%)
  blocking collectives  36.1 us (10%)
  matrix products  33.3 us (10%)
  other arithmetic  14.8 us (4%)
  between operations  13.5 us (4%)
    reduce_scatter x1, waiting for transfers between devices, on_device(): lax.psum_scatter(jnp.dot(attn, w_out, preferred_element_type=jnp.float32)...  165 us
    all_gather x1, waiting for transfers between devices, on_device(): carry_in = lax.all_gather(spare, 'blk', axis=0, tiled=True)  47.2 us
    all_to_all x1, blocking collectives, on_device(): local = lax.all_to_all(qkv, 'tile', split_axis=2, concat_axis=1, tiled=True)  36.1 us
    unnamed x7, local copies, waits for them, and re-layouts  17.2 us
    dot_general x8, matrix products, advance(): jnp.einsum('qd,kd->qk', queries, key_block, preferred_element_type=jnp.fl...  14.7 us
    dot_general x8, matrix products, advance(): jnp.dot(weights.astype(jnp.bfloat16), value_block, preferred_element_type...  12 us
    reduce_sum x8, other arithmetic, advance(): new_sum = run_sum * factor + jnp.sum(weights, axis=1)  7.81 us
  transfers between devices with their start and end apart: 2, of which 2 were waited for; matrix products, arithmetic and copies ran while one was open for 0% of the time, Pallas kernels for 0%

profile of v1, /device:TPU:2, one launch (start us, length us, event | category | flops | bytes accessed | tf_op | source)
XLA Modules:
  0.0 348.0 jit_solution(6897579178553892683)
XLA Ops:
  6.5 6.1 %copy.17 = bf16[3,32,4096]{1,0,2:T(4,128)(2,1)} copy(bf16[3,32,4096]{2,1,0:T(8,128)(2,1)} %param.5) | data formatting | bytes 1572864 | tf_op args[0]
  12.6 6.2 %reshape.88 = bf16[32,2,6144]{2,1,0:T(2,128)(2,1)S(1)} reshape(bf16[4096,3,32]{2,1,0:T(4,128)(2,1)} %bitcast.49) | data formatting | bytes 1572864
  18.8 36.1 %all_to_all.15 = bf16[32,2,6144]{2,1,0:T(2,128)(2,1)S(1)} all-to-all(bf16[32,2,6144]{2,1,0:T(2,128)(2,1)S(1)} %reshape.88), channel_id=1, replica_groups=mesh['blk'=8,'tile'=32] {'tile'}, dimensions={0} | all-to-all | bytes 1572864 | tf_op jit(solution)/shard_map/all_to_all | solution.py:24
  55.0 4.9 %reshape.89 = bf16[4096,3,32]{2,1,0:T(4,128)(2,1)} reshape(bf16[32,2,6144]{2,1,0:T(2,128)(2,1)S(1)} %all_to_all.15) | data formatting | bytes 1572864
  59.8 4.2 %copy.22 = bf16[3,32,32,128]{3,2,1,0:T(8,128)(2,1)S(1)} copy(bf16[3,32,32,128]{1,0,3,2:T(4,128)(2,1)} %bitcast.48) | data formatting | bytes 1572864 | tf_op jit(solution)/shard_map/all_to_all | solution.py:24
  66.2 47.2 %all-gather.2.cloned.1.call-done = bf16[8192,256]{1,0:T(8,128)(2,1)} async-done(((bf16[1024,256]{1,0:T(8,128)(2,1)}), bf16[8192,256]{1,0:T(8,128)(2,1)}) %all-gather.2.cloned.1.call-update) | async-done | bytes 4194320 | tf_op jit(solution)/shard_map/all_gather | solution.py:37
  113.4 3.8 %fusion.38 = (bf16[8192,128]{1,0:T(8,128)(2,1)S(1)}, bf16[8192,128]{1,0:T(8,128)(2,1)}) fusion(bf16[8192,256]{1,0:T(8,128)(2,1)} %all-gather.2.cloned.1.call-done), kind=kLoop, calls=%fused_computation.70 | loop fusion | bytes 8388608 | tf_op jit(solution)/shard_map/split | solution.py:38
  117.2 52.7 %while.18 = (s32[]{:T(128)}, f32[1024]{0:T(1024)S(1)}, f32[1024]{0:T(1024)S(1)}, f32[1024,128]{1,0:T(8,128)}, s32[1024]{0:T(1024)S(1)}, /*index=5*/s32[8]{0:T(12...) while((s32[]{:T(128)}, f32[1024]{0:T(1024)S(1)}, ...), condition=%wide.region_5.6_spmd.clone, body=%wide.region_1.5_spmd.clone.sunk | while | flops 552039424 | bytes 18714904 | solution.py:65
  118.6 1.8 fusion.54
  121.5 1.5 fusion.57
  125.2 1.8 fusion.54
  128.1 1.5 fusion.57
  131.8 1.8 fusion.54
  134.7 1.5 fusion.57
  138.4 1.8 fusion.54
  141.3 1.5 fusion.57
  145.0 1.8 fusion.54
  147.8 1.5 fusion.57
  151.6 1.8 fusion.54
  158.2 1.8 fusion.54
  164.7 1.8 fusion.54
  167.6 1.5 fusion.57
  169.9 6.6 %convolution_convert_fusion = bf16[1024,5120]{1,0:T(8,128)(2,1)} fusion(bf16[128,5120]{1,0:T(8,128)(2,1)S(1)} %copy-done, f32[1024,128]{1,0:T(8,128)} %get-tuple-element.169, f32[1024]{0:T(1024)S(1)} %get-tuple-element.170), kind=kOutput, calls=%fused_computation.49 | convolution fusion | flops 1347682304 | bytes 12324864 | tf_op jit(solution)/shard_map/dot_general | solution.py:69
  176.6 164.6 %reduce-scatter.2.cloned.1.call-done = bf16[32,5120]{1,0:T(8,128)(2,1)} async-done(((bf16[1024,5120]{1,0:T(8,128)(2,1)}), bf16[32,5120]{1,0:T(8,128)(2,1)}) %reduce-scatter.2.cloned.1.call-update) | async-done | bytes 327696 | tf_op jit(solution)/shard_map/reduce_scatter | solution.py:68
  (109 shorter events, 30.6 us)
Async XLA Ops:
  6.5 163.4 %copy-start = (bf16[128,5120]{1,0:T(8,128)(2,1)S(1)}, bf16[128,5120]{1,0:T(8,128)(2,1)}, u32[]{:S(2)}) copy-start(bf16[128,5120]{1,0:T(8,128)(2,1)} %param.7) | copy-start | bytes 3932164
  6.5 106.9 %all-gather.2.cloned.1.call-start = ((), (), s32[]{:S(2)}) async-start(), calls=%async_computation.2 | async-start | bytes 4718592 | tf_op jit(solution)/shard_map/all_gather | solution.py:37
  59.8 5.5 %copy-start.3 = (s32[16]{0:T(128)S(1)}, s32[16]{0:T(128)}, u32[]{:S(2)}) copy-start(s32[16]{0:T(128)} %param.6) | copy-start | bytes 196
  65.2 275.9 %reduce-scatter.2.cloned.1.call-start = ((), (), s32[]{:S(2)}) async-start(), calls=%async_computation.3 | async-start | bytes 10813440 | tf_op jit(solution)/shard_map/reduce_scatter | solution.py:68
  118.6 2.9 copy-start.1
  123.0 0.8 copy-start.2
  125.2 2.9 copy-start.1
  129.6 0.8 copy-start.2
  131.8 2.9 copy-start.1
  136.2 0.8 copy-start.2
  138.4 2.9 copy-start.1
  142.8 0.8 copy-start.2
  145.0 2.9 copy-start.1
  149.3 0.8 copy-start.2
  151.6 2.9 copy-start.1
  155.9 0.8 copy-start.2
  158.1 2.9 copy-start.1
  162.5 0.8 copy-start.2
  164.7 2.9 copy-start.1
  169.1 0.8 copy-start.2
Sparse Core Ops, SparseCore 0:
  65.3 48.0 all-gather.1
  176.7 164.4 reduce-scatter.1

commit v2 on v0

--- a/solution.py
+++ b/solution.py
@@ -33,7 +33,10 @@
         jnp.zeros((tok_blk, head_dim), jnp.float32),
     )
     carry = start_state
-    key_piece = lax.all_gather(keys_all, "blk", axis=0, tiled=True)
+    peers = lax.axis_size("blk")
+    blocks = jnp.stack([keys_all for _ in range(peers)])
+    blocks = lax.all_to_all(blocks, "blk", split_axis=0, concat_axis=0)
+    key_piece = jnp.concatenate(blocks, axis=0)
     value_piece = lax.all_gather(values_all, "blk", axis=0, tiled=True)
     count = key_piece.shape[0]
     width = math.gcd(count, tok_blk)

time: 376 us -> 361 us (0.960)
  waiting for transfers between devices: 246 us -> 214 us
  local copies, waits for them, and re-layouts: 27.9 us -> 37.4 us
  starting transfers between devices: 0.09 us -> 4.95 us
    all_gather x1 -> x0, waiting for transfers between devices: 45.2 us -> none  [on_device(): key_piece = lax.all_gather(keys_all, 'blk', axis=0, tiled=True)]
    all_to_all x0 -> x1, waiting for transfers between devices: none -> 30.8 us  [on_device(): blocks = lax.all_to_all(blocks, 'blk', split_axis=0, concat_axis=0)]
    all_gather x1, waiting for transfers between devices: 35.8 us -> 19.4 us  [on_device(): value_piece = lax.all_gather(values_all, 'blk', axis=0, tiled=True)]
    while x8 -> x40, local copies, waits for them, and re-layouts: 0.02 us -> 6.45 us
    all_to_all x0 -> x1, starting transfers between devices: none -> 4.94 us  [on_device(): blocks = lax.all_to_all(blocks, 'blk', split_axis=0, concat_axis=0)]
  transfers between devices with their start and end apart: 3 -> 3, of which waited for: 3 -> 3; matrix products, arithmetic and copies ran while one was open for 0% -> 1% of each run, Pallas kernels for 0% -> 0%
where the time goes in v2:
time: 361 us; the launch traced here: 360 us
  waiting for transfers between devices  214 us (59%)
  matrix products  39 us (11%)
  local copies, waits for them, and re-layouts  37.4 us (10%)
  blocking collectives  36.1 us (10%)
  other arithmetic  14 us (4%)
  between operations  13.5 us (4%)
  starting transfers between devices  4.95 us (1%)
    reduce_scatter x1, waiting for transfers between devices, on_device(): lax.psum_scatter(jnp.dot(attn, w_out, preferred_element_type=jnp.float32)...  164 us
    all_to_all x1, blocking collectives, on_device(): local = lax.all_to_all(qkv, 'tile', split_axis=2, concat_axis=1, tiled=True)  36.1 us
    all_to_all x1, waiting for transfers between devices, on_device(): blocks = lax.all_to_all(blocks, 'blk', split_axis=0, concat_axis=0)  30.8 us
    all_gather x1, waiting for transfers between devices, on_device(): value_piece = lax.all_gather(values_all, 'blk', axis=0, tiled=True)  19.4 us
    dot_general x8, matrix products, advance(): jnp.dot(weights.astype(jnp.bfloat16), value_block, preferred_element_type...  18.4 us
    unnamed x7, local copies, waits for them, and re-layouts  17.1 us
    dot_general x8, matrix products, advance(): jnp.einsum('qd,kd->qk', queries, key_block, preferred_element_type=jnp.fl...  14 us
    reduce_sum x8, other arithmetic, advance(): new_sum = run_sum * factor + jnp.sum(weights, axis=1)  7.81 us
  transfers between devices with their start and end apart: 3, of which 3 were waited for; matrix products, arithmetic and copies ran while one was open for 1% of the time, Pallas kernels for 0%

profile of v2, /device:TPU:2, one launch (start us, length us, event | category | flops | bytes accessed | tf_op | source)
XLA Modules:
  0.0 359.7 jit_solution(9354017206300492714)
XLA Ops:
  6.5 6.1 %copy.17 = bf16[3,32,4096]{1,0,2:T(4,128)(2,1)} copy(bf16[3,32,4096]{2,1,0:T(8,128)(2,1)} %param.5) | data formatting | bytes 1572864 | tf_op args[0]
  12.6 6.2 %reshape.85 = bf16[32,2,6144]{2,1,0:T(2,128)(2,1)S(1)} reshape(bf16[4096,3,32]{2,1,0:T(4,128)(2,1)} %bitcast.48) | data formatting | bytes 1572864
  18.8 36.1 %all_to_all.20 = bf16[32,2,6144]{2,1,0:T(2,128)(2,1)S(1)} all-to-all(bf16[32,2,6144]{2,1,0:T(2,128)(2,1)S(1)} %reshape.85), channel_id=1, replica_groups=mesh['blk'=8,'tile'=32] {'tile'}, dimensions={0} | all-to-all | bytes 1572864 | tf_op jit(solution)/shard_map/all_to_all | solution.py:24
  54.9 4.8 %reshape.86 = bf16[4096,3,32]{2,1,0:T(4,128)(2,1)} reshape(bf16[32,2,6144]{2,1,0:T(2,128)(2,1)S(1)} %all_to_all.20) | data formatting | bytes 1572864
  59.8 4.2 %copy.22 = bf16[3,32,32,128]{3,2,1,0:T(8,128)(2,1)S(1)} copy(bf16[3,32,32,128]{1,0,3,2:T(4,128)(2,1)} %bitcast.47) | data formatting | bytes 1572864 | tf_op jit(solution)/shard_map/all_to_all | solution.py:24
  67.3 4.9 %all-to-all-start.1 = ((bf16[8,1024,128]{2,1,0:T(8,128)(2,1)}), bf16[8,1024,128]{2,1,0:T(8,128)(2,1)S(1)}, u32[]{:S(2)}, u32[]{:S(2)}) async-start(bf16[8,1024,128]{2,1,0:T(8,128)(2,1)} %stack.3), calls=%async_computation.1 | async-start | bytes 4194304 | tf_op jit(solution)/shard_map/all_to_all | solution.py:38
  74.1 30.8 %all-to-all-done.1 = bf16[8,1024,128]{2,1,0:T(8,128)(2,1)S(1)} async-done(((bf16[8,1024,128]{2,1,0:T(8,128)(2,1)}), bf16[8,1024,128]{2,1,0:T(8,128)(2,1)S(1)}, u32[]{:S(2)}, u32[]{:S(2)}) %all-to-all-start.1) | async-done | bytes 2097184 | tf_op jit(solution)/shard_map/all_to_all | solution.py:38
  104.9 19.4 %all-gather.2.cloned.1.call-done = bf16[8192,128]{1,0:T(8,128)(2,1)} async-done(((bf16[1024,128]{1,0:T(8,128)(2,1)}), bf16[8192,128]{1,0:T(8,128)(2,1)}) %all-gather.2.cloned.1.call-update) | async-done | bytes 2097168 | tf_op jit(solution)/shard_map/all_gather | solution.py:40
  124.3 58.0 %while.18 = (s32[]{:T(128)}, f32[1024]{0:T(1024)S(1)}, f32[1024]{0:T(1024)S(1)}, f32[1024,128]{1,0:T(8,128)}, s32[1024]{0:T(1024)S(1)}, /*index=5*/s32[8]{0:T(12...) while((s32[]{:T(128)}, f32[1024]{0:T(1024)S(1)}, ...), condition=%wide.region_5.6_spmd.clone, body=%wide.region_1.5_spmd.clone.sunk | while | flops 552039424 | bytes 18714904 | solution.py:67
  128.4 2.3 fusion.56
  132.9 1.8 fusion.53
  135.7 2.3 fusion.56
  140.1 1.8 fusion.53
  142.9 2.3 fusion.56
  147.4 1.8 fusion.53
  150.2 2.3 fusion.56
  157.4 2.3 fusion.56
  161.9 1.8 fusion.53
  164.7 2.3 fusion.56
  171.9 2.3 fusion.56
  176.4 1.8 fusion.53
  179.2 2.3 fusion.56
  182.3 6.6 %convolution_convert_fusion = bf16[1024,5120]{1,0:T(8,128)(2,1)} fusion(bf16[128,5120]{1,0:T(8,128)(2,1)S(1)} %copy-done, f32[1024,128]{1,0:T(8,128)} %get-tuple-element.169, f32[1024]{0:T(1024)S(1)} %get-tuple-element.170), kind=kOutput, calls=%fused_computation.49 | convolution fusion | flops 1347682304 | bytes 12324864 | tf_op jit(solution)/shard_map/dot_general | solution.py:71
  189.0 163.9 %reduce-scatter.2.cloned.1.call-done = bf16[32,5120]{1,0:T(8,128)(2,1)} async-done(((bf16[1024,5120]{1,0:T(8,128)(2,1)}), bf16[32,5120]{1,0:T(8,128)(2,1)}) %reduce-scatter.2.cloned.1.call-update) | async-done | bytes 327696 | tf_op jit(solution)/shard_map/reduce_scatter | solution.py:70
  (110 shorter events, 35.4 us)
Async XLA Ops:
  6.5 175.8 %copy-start = (bf16[128,5120]{1,0:T(8,128)(2,1)S(1)}, bf16[128,5120]{1,0:T(8,128)(2,1)}, u32[]{:S(2)}) copy-start(bf16[128,5120]{1,0:T(8,128)(2,1)} %param.7) | copy-start | bytes 3932164
  6.5 117.8 %all-gather.2.cloned.1.call-start = ((), (), s32[]{:S(2)}) async-start(), calls=%async_computation.3 | async-start | bytes 2359296 | tf_op jit(solution)/shard_map/all_gather | solution.py:40
  64.8 7.5 %copy-start.3 = (s32[16]{0:T(128)S(1)}, s32[16]{0:T(128)}, u32[]{:S(2)}) copy-start(s32[16]{0:T(128)} %param.6) | copy-start | bytes 196
  67.3 37.6 %all-to-all-start.1 = ((bf16[8,1024,128]{2,1,0:T(8,128)(2,1)}), bf16[8,1024,128]{2,1,0:T(8,128)(2,1)S(1)}, u32[]{:S(2)}, u32[]{:S(2)}) async-start(bf16[8,1024,128]{2,1,0:T(8,128)(2,1)} %stack.3), calls=%async_computation.1 | async-start | bytes 4194304 | tf_op jit(solution)/shard_map/all_to_all | solution.py:38
  72.2 280.7 %reduce-scatter.2.cloned.1.call-start = ((), (), s32[]{:S(2)}) async-start(), calls=%async_computation.4 | async-start | bytes 10813440 | tf_op jit(solution)/shard_map/reduce_scatter | solution.py:70
  125.6 2.8 copy-start.1
  130.7 0.8 copy-start.2
  132.9 2.8 copy-start.1
  138.0 0.8 copy-start.2
  140.1 2.8 copy-start.1
  145.2 0.8 copy-start.2
  147.4 2.8 copy-start.1
  152.5 0.8 copy-start.2
  154.6 2.8 copy-start.1
  159.7 0.8 copy-start.2
  161.9 2.8 copy-start.1
  167.0 0.8 copy-start.2
  169.1 2.8 copy-start.1
  174.2 0.8 copy-start.2
  176.4 2.8 copy-start.1
  181.5 0.8 copy-start.2
Sparse Core Ops, SparseCore 0:
  65.7 58.5 all-gather.1
  189.1 163.7 reduce-scatter.1
